TPU v7x, 256 devices: a whole 4x4x8 slice. The times are simulated.
256 devices in a mesh: row: 32 (over x, z), col: 8 (over y, core).
Axes of the slice: x: 4, y: 4, z: 8, core: 2. Of those that a mesh axis runs over, the one named last changes fastest.
Arguments:
- panel_block: float32 [16384, 128], P('row'), may hold values from -8 to 8, as said below
- trailing: float32 [16384, 16384], P('row', 'col'), may hold values from -80 to 80
Outputs:
- reduced: float32 [16384, 16384], P('row', 'col')
- band_block: float32 [128, 128], replicated
- first_factor: float32 [128, 128], replicated
Inputs may be any that keep to these rules, and one draw needn't show every extreme that they name: `panel_block`: entries of order the inverse square root of 16384; rows may differ in scale; the columns may be nearly dependent, with a condition number of the panel up to a few thousand; the first 128 rows of the orthonormal basis have spectral norm at most 0.8, so that I + top^T needs no pivoting.
All inputs are finite; a program needn't handle non-finite values.
Results may differ from a plain program's by a relative error of at most 0.0017.
Values sent between devices are 32-bit elements; how exact they have to be, the bound alone decides.
A program may use at most 128 MiB of HBM per device.

v0:
```python
import jax
import jax.numpy as jnp
from jax import lax
from jax.sharding import PartitionSpec as P

HIGH = lax.Precision.HIGHEST


def broadcast(shard, axis, root):
    mine = lax.axis_index(axis) == root
    return lax.psum(jnp.where(mine, shard, jnp.zeros_like(shard)), axis)


def gram_of(values):
    return lax.dot_general(
        values, values, (((0,), (0,)), ((), ())), precision=HIGH, preferred_element_type=jnp.float32
    )


def times_of(left, right):
    return jnp.dot(left, right, precision=HIGH, preferred_element_type=jnp.float32)


def outer_of(left, right):
    return lax.dot_general(
        left, right, (((1,), (1,)), ((), ())), precision=HIGH, preferred_element_type=jnp.float32
    )


def gram_both(left, right):
    return lax.dot_general(
        left, right, (((0,), (0,)), ((), ())), precision=HIGH, preferred_element_type=jnp.float32
    )


def eliminate_small(square):
    size_n = square.shape[0]
    augmented = jnp.concatenate([square, jnp.eye(size_n, dtype=square.dtype)], axis=1)
    positions = jnp.arange(size_n)

    def eliminate(pivot, current):
        pivot_row = lax.dynamic_index_in_dim(current, pivot, 0, keepdims=False)
        pivot_row = pivot_row / pivot_row[pivot]
        column = lax.dynamic_index_in_dim(current, pivot, 1, keepdims=False)
        column = column - (positions == pivot).astype(current.dtype)
        return current - column[:, None] * pivot_row[None, :]

    augmented = lax.fori_loop(0, size_n, eliminate, augmented)
    return augmented[:, size_n:]


def invert_square(square):
    size_n = square.shape[0]
    if size_n <= 16:
        return eliminate_small(square)
    half = size_n // 2
    upper_left = square[:half, :half]
    upper_right = square[:half, half:]
    lower_left = square[half:, :half]
    lower_right = square[half:, half:]
    left_inverse = invert_square(upper_left)
    left_times_right = times_of(left_inverse, upper_right)
    lower_times_left = times_of(lower_left, left_inverse)
    schur = lower_right - times_of(lower_left, left_times_right)
    schur_inverse = invert_square(schur)
    top_right = -times_of(left_times_right, schur_inverse)
    bottom_left = -times_of(schur_inverse, lower_times_left)
    top_left = left_inverse - times_of(top_right, lower_times_left)
    upper = jnp.concatenate([top_left, top_right], axis=1)
    lower = jnp.concatenate([bottom_left, schur_inverse], axis=1)
    return jnp.concatenate([upper, lower], axis=0)


def right_solve(factor, values):
    return lax.linalg.triangular_solve(
        factor, values, left_side=False, lower=True, transpose_a=True
    )


def body(panel_block, trailing):
    shard_rows = panel_block.shape[0]
    panel_width = panel_block.shape[1]
    col_count = trailing.shape[1]
    row_index = lax.axis_index("row")
    col_index = lax.axis_index("col")
    first_gram = lax.psum(gram_of(panel_block), "row")
    first_factor = jnp.linalg.cholesky(first_gram)
    first_basis = right_solve(first_factor, panel_block)
    second_gram = lax.psum(gram_of(first_basis), "row")
    second_factor = jnp.linalg.cholesky(second_gram)
    basis = right_solve(second_factor, first_basis)
    top_basis = broadcast(basis[:panel_width], "row", 0)
    band_block = -times_of(second_factor.T, first_factor.T)
    kernel = invert_square(jnp.eye(panel_width, dtype=jnp.float32) + top_basis.T)
    global_rows = row_index * shard_rows + jnp.arange(shard_rows)
    ident = (global_rows[:, None] == jnp.arange(panel_width)[None, :]).astype(jnp.float32)
    vectors = basis + ident
    all_vectors = lax.all_gather(vectors, "row", axis=0, tiled=True)
    col_vectors = lax.dynamic_slice_in_dim(all_vectors, col_index * col_count, col_count, 0)
    partial_product = times_of(trailing, col_vectors)
    row_product = lax.psum(partial_product, "col")
    applied = times_of(row_product, kernel)
    inner_sum = lax.psum(gram_both(vectors, applied), "row")
    inner = times_of(kernel.T, inner_sum)
    row_update = applied - 0.5 * times_of(vectors, inner)
    all_update = lax.all_gather(row_update, "row", axis=0, tiled=True)
    col_update = lax.dynamic_slice_in_dim(all_update, col_index * col_count, col_count, 0)
    reduced = trailing - outer_of(vectors, col_update) - outer_of(row_update, col_vectors)
    return (reduced, band_block, first_factor)


def solution(mesh):
    in_specs = (P("row", None), P("row", "col"))
    out_specs = (P("row", "col"), P(), P())
    return jax.shard_map(body, mesh=mesh, in_specs=in_specs, out_specs=out_specs, check_vma=False)
```

profile of v0, /device:TPU:1, one launch (start us, length us, event | category | flops | bytes accessed | tf_op | source)
XLA Modules:
  0.0 1025.3 jit_solution(8369350252822602380)
XLA Ops:
  9.4 143.5 %all-reduce.6.cloned.1.call-done = f32[128,128]{0,1:T(8,128)} async-done(((f32[128,128]{0,1:T(8,128)}), f32[128,128]{0,1:T(8,128)}) %all-reduce.6.cloned.1.call-update) | async-done | bytes 65552 | tf_op jit(solution)/shard_map/psum | solution.py:86
  154.7 11.7 %cholesky.44 = f32[128,128]{1,0:T(8,128)S(1)} custom-call(f32[128,128]{1,0:T(8,128)S(1)} %fusion.57), custom_call_target="Cholesky" | custom-call | tf_op jit(solution)/shard_map/jit(cholesky)/cholesky | solution.py:87
  167.8 9.8 custom-call.6
  179.3 139.5 %all-reduce.8.cloned.1.call-done = f32[128,128]{0,1:T(8,128)} async-done(((f32[128,128]{0,1:T(8,128)}), f32[128,128]{0,1:T(8,128)}) %all-reduce.8.cloned.1.call-update) | async-done | bytes 65552 | tf_op jit(solution)/shard_map/psum | solution.py:89
  320.6 11.7 %cholesky.55 = f32[128,128]{1,0:T(8,128)S(1)} custom-call(f32[128,128]{1,0:T(8,128)S(1)} %fusion.55), custom_call_target="Cholesky" | custom-call | tf_op jit(solution)/shard_map/jit(cholesky)/cholesky | solution.py:90
  333.5 9.8 custom-call.7
  346.0 138.9 %all-reduce.12.cloned.1.call-done = f32[128,128]{1,0:T(8,128)} async-done(((f32[128,128]{1,0:T(8,128)}), f32[128,128]{1,0:T(8,128)}) %all-reduce.12.cloned.1.call-update) | async-done | bytes 65552 | tf_op jit(solution)/shard_map/psum | solution.py:11
  485.9 24.0 %while.136 = (s32[]{:T(128)}, f32[16,32]{0,1:T(8,128)S(1)}, s32[]{:T(128)}, s32[]{:T(128)}, s32[]{:T(128)}, /*index=5*/s32[]{:T(128)}) while((s32[]{:T(128)}, f32[16,32]{0,1:T(8,128)S(1)}, s32[]{:T(128)}, s32[]{:T(128)}, s32[]{:T(128)}, /*index=5*/s32[]{:T(128)}) %tuple.325), condition=%wide.region_7.10_spmd.clone, body=%wide.region_6.9_spmd.clone.sunk | while | flops 1108 | bytes 5825 | solution.py:48
  510.8 24.0 %while.137 = (s32[]{:T(128)}, f32[16,32]{0,1:T(8,128)S(1)}, s32[]{:T(128)}, s32[]{:T(128)}, s32[]{:T(128)}, /*index=5*/s32[]{:T(128)}) while((s32[]{:T(128)}, f32[16,32]{0,1:T(8,128)S(1)}, s32[]{:T(128)}, s32[]{:T(128)}, s32[]{:T(128)}, /*index=5*/s32[]{:T(128)}) %tuple.328), condition=%wide.region_9.12_spmd.clone, body=%wide.region_8.11_spmd.clone.sunk | while | flops 1108 | bytes 5825 | solution.py:48
  536.2 24.0 %while.138 = (s32[]{:T(128)}, f32[16,32]{0,1:T(8,128)S(1)}, s32[]{:T(128)}, s32[]{:T(128)}, s32[]{:T(128)}, /*index=5*/s32[]{:T(128)}) while((s32[]{:T(128)}, f32[16,32]{0,1:T(8,128)S(1)}, s32[]{:T(128)}, s32[]{:T(128)}, s32[]{:T(128)}, /*index=5*/s32[]{:T(128)}) %tuple.331), condition=%wide.region_11.14_spmd.clone, body=%wide.region_10.13_spmd.clone.sunk | while | flops 1108 | bytes 5825 | solution.py:48
  561.1 24.0 %while.139 = (s32[]{:T(128)}, f32[16,32]{0,1:T(8,128)S(1)}, s32[]{:T(128)}, s32[]{:T(128)}, s32[]{:T(128)}, /*index=5*/s32[]{:T(128)}) while((s32[]{:T(128)}, f32[16,32]{0,1:T(8,128)S(1)}, s32[]{:T(128)}, s32[]{:T(128)}, s32[]{:T(128)}, /*index=5*/s32[]{:T(128)}) %tuple.334), condition=%wide.region_13.16_spmd.clone, body=%wide.region_12.15_spmd.clone.sunk | while | flops 1108 | bytes 5825 | solution.py:48
  587.1 24.0 %while.140 = (s32[]{:T(128)}, f32[16,32]{0,1:T(8,128)S(1)}, s32[]{:T(128)}, s32[]{:T(128)}, s32[]{:T(128)}, /*index=5*/s32[]{:T(128)}) while((s32[]{:T(128)}, f32[16,32]{0,1:T(8,128)S(1)}, s32[]{:T(128)}, s32[]{:T(128)}, s32[]{:T(128)}, /*index=5*/s32[]{:T(128)}) %tuple.337), condition=%wide.region_15.18_spmd.clone, body=%wide.region_14.17_spmd.clone.sunk | while | flops 1108 | bytes 5825 | solution.py:48
  611.7 24.0 %while.141 = (s32[]{:T(128)}, f32[16,32]{0,1:T(8,128)S(1)}, s32[]{:T(128)}, s32[]{:T(128)}, s32[]{:T(128)}, /*index=5*/s32[]{:T(128)}) while((s32[]{:T(128)}, f32[16,32]{0,1:T(8,128)S(1)}, s32[]{:T(128)}, s32[]{:T(128)}, s32[]{:T(128)}, /*index=5*/s32[]{:T(128)}) %tuple.340), condition=%wide.region_17.20_spmd.clone, body=%wide.region_16.19_spmd.clone.sunk | while | flops 1108 | bytes 5825 | solution.py:48
  637.1 24.0 %while.142 = (s32[]{:T(128)}, f32[16,32]{0,1:T(8,128)S(1)}, s32[]{:T(128)}, s32[]{:T(128)}, s32[]{:T(128)}, /*index=5*/s32[]{:T(128)}) while((s32[]{:T(128)}, f32[16,32]{0,1:T(8,128)S(1)}, s32[]{:T(128)}, s32[]{:T(128)}, s32[]{:T(128)}, /*index=5*/s32[]{:T(128)}) %tuple.343), condition=%wide.region_19.22_spmd.clone, body=%wide.region_18.21_spmd.clone.sunk | while | flops 1108 | bytes 5825 | solution.py:48
  661.7 24.0 %while.143 = (s32[]{:T(128)}, f32[16,32]{0,1:T(8,128)S(1)}, s32[]{:T(128)}, s32[]{:T(128)}, s32[]{:T(128)}, /*index=5*/s32[]{:T(128)}) while((s32[]{:T(128)}, f32[16,32]{0,1:T(8,128)S(1)}, s32[]{:T(128)}, s32[]{:T(128)}, s32[]{:T(128)}, /*index=5*/s32[]{:T(128)}) %tuple.346), condition=%wide.region_21.24_spmd.clone, body=%wide.region_20.23_spmd.clone.sunk | while | flops 1108 | bytes 5825 | solution.py:48
  688.1 7.6 convolution_bitcast_fusion
  696.0 65.7 %all-reduce.10.cloned.1.call-done = f32[512,128]{0,1:T(8,128)} async-done(((f32[512,128]{0,1:T(8,128)}), f32[512,128]{0,1:T(8,128)}) %all-reduce.10.cloned.1.call-update) | async-done | bytes 262160 | tf_op jit(solution)/shard_map/psum | solution.py:101
  761.7 1.6 fusion.132
  764.6 139.2 %all-reduce.14.cloned.1.call-done = f32[128,128]{1,0:T(8,128)} async-done(((f32[128,128]{1,0:T(8,128)}), f32[128,128]{1,0:T(8,128)}) %all-reduce.14.cloned.1.call-update) | async-done | bytes 65552 | tf_op jit(solution)/shard_map/psum | solution.py:103
  905.1 1.3 fusion.48
  906.4 1.5 convolution_negate_fusion
  907.9 98.7 %all-gather.5.cloned.1.call-done = f32[16384,128]{1,0:T(8,128)} async-done(((f32[512,128]{1,0:T(8,128)}), f32[16384,128]{1,0:T(8,128)}) %all-gather.5.cloned.1.call-update) | async-done | bytes 8388624 | tf_op jit(solution)/shard_map/all_gather | solution.py:106
  1006.7 5.0 fusion.49
  1011.7 6.7 subtract_subtract_fusion
  (632 shorter events, 217.4 us)
Async XLA Ops:
  7.2 1.0 copy-start
  7.2 145.8 %all-reduce.6.cloned.1.call-start = ((), (), s32[]{:S(2)}) async-start(), calls=%async_computation | async-start | bytes 131072 | tf_op jit(solution)/shard_map/psum | solution.py:86
  9.4 309.4 %all-reduce.8.cloned.1.call-start = ((), (), s32[]{:S(2)}) async-start(), calls=%async_computation.1 | async-start | bytes 131072 | tf_op jit(solution)/shard_map/psum | solution.py:89
  167.8 738.6 %copy-start.4 = (f32[128,128]{1,0:T(8,128)}, f32[128,128]{1,0:T(8,128)S(1)}, u32[]{:S(2)}) copy-start(f32[128,128]{1,0:T(8,128)S(1)} %get-tuple-element.926) | copy-start | bytes 196612
  179.1 305.8 %all-reduce.12.cloned.1.call-start = ((), (), s32[]{:S(2)}) async-start(), calls=%async_computation.4 | async-start | bytes 131072 | tf_op jit(solution)/shard_map/psum | solution.py:11
  345.1 343.0 %all-gather.3.cloned.1.call-start = ((), (), s32[]{:S(2)}) async-start(), calls=%async_computation.2 | async-start | bytes 8650752 | tf_op jit(solution)/shard_map/all_gather | solution.py:98
  345.7 416.0 %all-reduce.10.cloned.1.call-start = ((), (), s32[]{:S(2)}) async-start(), calls=%async_computation.3 | async-start | bytes 524288 | tf_op jit(solution)/shard_map/psum | solution.py:101
  637.1 126.1 %copy-start.2 = (f32[512,128]{0,1:T(8,128)S(1)}, f32[512,128]{0,1:T(8,128)}, u32[]{:S(2)}) copy-start(f32[512,128]{0,1:T(8,128)} %get-tuple-element.927) | copy-start | bytes 786436
  695.7 208.2 %all-reduce.14.cloned.1.call-start = ((), (), s32[]{:S(2)}) async-start(), calls=%async_computation.5 | async-start | bytes 131072 | tf_op jit(solution)/shard_map/psum | solution.py:103
  764.3 242.3 %all-gather.5.cloned.1.call-start = ((), (), s32[]{:S(2)}) async-start(), calls=%async_computation.6 | async-start | bytes 8650752 | tf_op jit(solution)/shard_map/all_gather | solution.py:106
  906.4 105.3 %copy-start.3 = (f32[512,128]{1,0:T(8,128)S(1)}, f32[512,128]{1,0:T(8,128)}, u32[]{:S(2)}) copy-start(f32[512,128]{1,0:T(8,128)} %fusion.48) | copy-start | bytes 786436
  1006.7 5.1 copy-start.1
Sparse Core Ops, SparseCore 0:
  12.0 140.8 all-reduce.5
  179.2 139.5 all-reduce.7
  345.3 139.6 all-reduce.11
  487.9 100.0 all-gather.2
  695.8 65.7 all-reduce.9
  765.6 138.2 all-reduce.13
  907.0 99.5 all-gather.4
where the time goes:
time: 1030 us
  waiting for transfers between devices  726 us (70%)
  other arithmetic  166 us (16%)
  local copies, waits for them, and re-layouts  79.2 us (8%)
  matrix products  37.4 us (4%)
  between operations  14.5 us (1%)
    psum x1, waiting for transfers between devices, body(): first_gram = lax.psum(gram_of(panel_block), 'row')  144 us
    psum x1, waiting for transfers between devices, body(): second_gram = lax.psum(gram_of(first_basis), 'row')  139 us
    psum x1, waiting for transfers between devices, body(): inner_sum = lax.psum(gram_both(vectors, applied), 'row')  139 us
    psum x1, waiting for transfers between devices, broadcast(): return lax.psum(jnp.where(mine, shard, jnp.zeros_like(shard)), axis)  139 us
    div x128, other arithmetic, eliminate(): pivot_row = pivot_row / pivot_row[pivot]  106 us
    all_gather x1, waiting for transfers between devices, body(): all_update = lax.all_gather(row_update, 'row', axis=0, tiled=True)  98.7 us
    dynamic_slice x128, local copies, waits for them, and re-layouts, eliminate(): pivot_row = pivot_row / pivot_row[pivot]  74.9 us
    psum x1, waiting for transfers between devices, body(): row_product = lax.psum(partial_product, 'col')  65.7 us
  transfers between devices with their start and end apart: 7, of which 6 were waited for; matrix products, arithmetic and copies ran while one was open for 20% of the time, Pallas kernels for 0%

commit v1 on v0

--- a/solution.py
+++ b/solution.py
@@ -86,7 +86,7 @@
     first_gram = lax.psum(gram_of(panel_block), "row")
     first_factor = jnp.linalg.cholesky(first_gram)
     first_basis = right_solve(first_factor, panel_block)
-    second_gram = lax.psum(gram_of(first_basis), "row")
+    second_gram = jnp.sum(lax.all_gather(gram_of(first_basis), "row"), axis=0)
     second_factor = jnp.linalg.cholesky(second_gram)
     basis = right_solve(second_factor, first_basis)
     top_basis = broadcast(basis[:panel_width], "row", 0)

time: 1030 us -> 962 us (0.934)
  waiting for transfers between devices: 726 us -> 662 us
    psum x1 -> x0, waiting for transfers between devices: 139 us -> none  [body(): second_gram = lax.psum(gram_of(first_basis), 'row')]
    all_gather x0 -> x1, waiting for transfers between devices: none -> 75.7 us  [body(): second_gram = jnp.sum(lax.all_gather(gram_of(first_basis), 'row'), axis=0)]
  transfers between devices with their start and end apart: 7 -> 7, of which waited for: 6 -> 6; matrix products, arithmetic and copies ran while one was open for 20% -> 21% of each run, Pallas kernels for 0% -> 0%
where the time goes in v1:
time: 962 us; the launch traced here: 961 us
  waiting for transfers between devices  662 us (69%)
  other arithmetic  167 us (17%)
  local copies, waits for them, and re-layouts  78.3 us (8%)
  matrix products  37.4 us (4%)
  between operations  14.5 us (2%)
    psum x1, waiting for transfers between devices, body(): first_gram = lax.psum(gram_of(panel_block), 'row')  144 us
    psum x1, waiting for transfers between devices, body(): inner_sum = lax.psum(gram_both(vectors, applied), 'row')  139 us
    psum x1, waiting for transfers between devices, broadcast(): return lax.psum(jnp.where(mine, shard, jnp.zeros_like(shard)), axis)  138 us
    div x128, other arithmetic, eliminate(): pivot_row = pivot_row / pivot_row[pivot]  106 us
    all_gather x1, waiting for transfers between devices, body(): all_update = lax.all_gather(row_update, 'row', axis=0, tiled=True)  98.7 us
    all_gather x1, waiting for transfers between devices, body(): second_gram = jnp.sum(lax.all_gather(gram_of(first_basis), 'row'), axis=0)  75.7 us
    dynamic_slice x128, local copies, waits for them, and re-layouts, eliminate(): pivot_row = pivot_row / pivot_row[pivot]  74.9 us
    psum x1, waiting for transfers between devices, body(): row_product = lax.psum(partial_product, 'col')  65.7 us
  transfers between devices with their start and end apart: 7, of which 6 were waited for; matrix products, arithmetic and copies ran while one was open for 21% of the time, Pallas kernels for 0%

profile of v1, /device:TPU:1, one launch (start us, length us, event | category | flops | bytes accessed | tf_op | source)
XLA Modules:
  0.0 960.8 jit_solution(15597322216782677483)
XLA Ops:
  9.4 143.5 %all-reduce.5.cloned.1.call-done = f32[128,128]{0,1:T(8,128)} async-done(((f32[128,128]{0,1:T(8,128)}), f32[128,128]{0,1:T(8,128)}) %all-reduce.5.cloned.1.call-update) | async-done | bytes 65552 | tf_op jit(solution)/shard_map/psum | solution.py:86
  154.7 11.7 %cholesky.44 = f32[128,128]{1,0:T(8,128)S(1)} custom-call(f32[128,128]{1,0:T(8,128)S(1)} %fusion.57), custom_call_target="Cholesky" | custom-call | tf_op jit(solution)/shard_map/jit(cholesky)/cholesky | solution.py:87
  167.8 9.8 %custom-call.6 = f32[1,128,128]{1,2,0:T(8,128)S(1)} custom-call(f32[1,128,128]{2,1,0:T(8,128)S(1)} %get-tuple-element.941), custom_call_target="InvertDiagBlocksLowerTriangular" | custom-call | tf_op jit(solution)/shard_map/triangular_solve/custom-call.0 | solution.py:75
  179.3 75.7 %all-gather.9.cloned.1.call-done = f32[4096,128]{1,0:T(8,128)} async-done(((f32[128,128]{1,0:T(8,128)}), f32[4096,128]{1,0:T(8,128)}) %all-gather.9.cloned.1.call-update) | async-done | bytes 2097168 | tf_op jit(solution)/shard_map/all_gather | solution.py:89
  255.0 1.7 reduce_sum.9
  256.8 11.7 %cholesky.55 = f32[128,128]{1,0:T(8,128)S(1)} custom-call(f32[128,128]{1,0:T(8,128)S(1)} %fusion.55), custom_call_target="Cholesky" | custom-call | tf_op jit(solution)/shard_map/jit(cholesky)/cholesky | solution.py:90
  269.8 9.8 %custom-call.7 = f32[1,128,128]{1,2,0:T(8,128)S(1)} custom-call(f32[1,128,128]{2,1,0:T(8,128)S(1)} %select_bitcast_fusion), custom_call_target="InvertDiagBlocksLowerTriangular" | custom-call | tf_op jit(solution)/shard_map/triangular_solve/custom-call.0 | solution.py:75
  282.2 138.2 %all-reduce.9.cloned.1.call-done = f32[128,128]{1,0:T(8,128)} async-done(((f32[128,128]{1,0:T(8,128)}), f32[128,128]{1,0:T(8,128)}) %all-reduce.9.cloned.1.call-update) | async-done | bytes 65552 | tf_op jit(solution)/shard_map/psum | solution.py:11
  421.5 24.0 %while.136 = (s32[]{:T(128)}, f32[16,32]{0,1:T(8,128)S(1)}, s32[]{:T(128)}, s32[]{:T(128)}, s32[]{:T(128)}, /*index=5*/s32[]{:T(128)}) while((s32[]{:T(128)}, f32[16,32]{0,1:T(8,128)S(1)}, s32[]{:T(128)}, s32[]{:T(128)}, s32[]{:T(128)}, /*index=5*/s32[]{:T(128)}) %tuple.333), condition=%wide.region_7.10_spmd.clone, body=%wide.region_6.9_spmd.clone.sunk | while | flops 1108 | bytes 5825 | solution.py:48
  446.3 24.0 %while.137 = (s32[]{:T(128)}, f32[16,32]{0,1:T(8,128)S(1)}, s32[]{:T(128)}, s32[]{:T(128)}, s32[]{:T(128)}, /*index=5*/s32[]{:T(128)}) while((s32[]{:T(128)}, f32[16,32]{0,1:T(8,128)S(1)}, s32[]{:T(128)}, s32[]{:T(128)}, s32[]{:T(128)}, /*index=5*/s32[]{:T(128)}) %tuple.336), condition=%wide.region_9.12_spmd.clone, body=%wide.region_8.11_spmd.clone.sunk | while | flops 1108 | bytes 5825 | solution.py:48
  471.8 24.0 %while.138 = (s32[]{:T(128)}, f32[16,32]{0,1:T(8,128)S(1)}, s32[]{:T(128)}, s32[]{:T(128)}, s32[]{:T(128)}, /*index=5*/s32[]{:T(128)}) while((s32[]{:T(128)}, f32[16,32]{0,1:T(8,128)S(1)}, s32[]{:T(128)}, s32[]{:T(128)}, s32[]{:T(128)}, /*index=5*/s32[]{:T(128)}) %tuple.339), condition=%wide.region_11.14_spmd.clone, body=%wide.region_10.13_spmd.clone.sunk | while | flops 1108 | bytes 5825 | solution.py:48
  496.6 24.0 %while.139 = (s32[]{:T(128)}, f32[16,32]{0,1:T(8,128)S(1)}, s32[]{:T(128)}, s32[]{:T(128)}, s32[]{:T(128)}, /*index=5*/s32[]{:T(128)}) while((s32[]{:T(128)}, f32[16,32]{0,1:T(8,128)S(1)}, s32[]{:T(128)}, s32[]{:T(128)}, s32[]{:T(128)}, /*index=5*/s32[]{:T(128)}) %tuple.342), condition=%wide.region_13.16_spmd.clone, body=%wide.region_12.15_spmd.clone.sunk | while | flops 1108 | bytes 5825 | solution.py:48
  522.6 24.0 %while.140 = (s32[]{:T(128)}, f32[16,32]{0,1:T(8,128)S(1)}, s32[]{:T(128)}, s32[]{:T(128)}, s32[]{:T(128)}, /*index=5*/s32[]{:T(128)}) while((s32[]{:T(128)}, f32[16,32]{0,1:T(8,128)S(1)}, s32[]{:T(128)}, s32[]{:T(128)}, s32[]{:T(128)}, /*index=5*/s32[]{:T(128)}) %tuple.345), condition=%wide.region_15.18_spmd.clone, body=%wide.region_14.17_spmd.clone.sunk | while | flops 1108 | bytes 5825 | solution.py:48
  547.2 24.0 %while.141 = (s32[]{:T(128)}, f32[16,32]{0,1:T(8,128)S(1)}, s32[]{:T(128)}, s32[]{:T(128)}, s32[]{:T(128)}, /*index=5*/s32[]{:T(128)}) while((s32[]{:T(128)}, f32[16,32]{0,1:T(8,128)S(1)}, s32[]{:T(128)}, s32[]{:T(128)}, s32[]{:T(128)}, /*index=5*/s32[]{:T(128)}) %tuple.348), condition=%wide.region_17.20_spmd.clone, body=%wide.region_16.19_spmd.clone.sunk | while | flops 1108 | bytes 5825 | solution.py:48
  572.7 24.0 %while.142 = (s32[]{:T(128)}, f32[16,32]{0,1:T(8,128)S(1)}, s32[]{:T(128)}, s32[]{:T(128)}, s32[]{:T(128)}, /*index=5*/s32[]{:T(128)}) while((s32[]{:T(128)}, f32[16,32]{0,1:T(8,128)S(1)}, s32[]{:T(128)}, s32[]{:T(128)}, s32[]{:T(128)}, /*index=5*/s32[]{:T(128)}) %tuple.351), condition=%wide.region_19.22_spmd.clone, body=%wide.region_18.21_spmd.clone.sunk | while | flops 1108 | bytes 5825 | solution.py:48
  597.3 24.0 %while.143 = (s32[]{:T(128)}, f32[16,32]{0,1:T(8,128)S(1)}, s32[]{:T(128)}, s32[]{:T(128)}, s32[]{:T(128)}, /*index=5*/s32[]{:T(128)}) while((s32[]{:T(128)}, f32[16,32]{0,1:T(8,128)S(1)}, s32[]{:T(128)}, s32[]{:T(128)}, s32[]{:T(128)}, /*index=5*/s32[]{:T(128)}) %tuple.354), condition=%wide.region_21.24_spmd.clone, body=%wide.region_20.23_spmd.clone.sunk | while | flops 1108 | bytes 5825 | solution.py:48
  623.7 7.6 convolution_bitcast_fusion
  631.5 65.7 %all-reduce.7.cloned.1.call-done = f32[512,128]{0,1:T(8,128)} async-done(((f32[512,128]{0,1:T(8,128)}), f32[512,128]{0,1:T(8,128)}) %all-reduce.7.cloned.1.call-update) | async-done | bytes 262160 | tf_op jit(solution)/shard_map/psum | solution.py:101
  697.2 1.6 fusion.132
  700.2 139.2 %all-reduce.11.cloned.1.call-done = f32[128,128]{1,0:T(8,128)} async-done(((f32[128,128]{1,0:T(8,128)}), f32[128,128]{1,0:T(8,128)}) %all-reduce.11.cloned.1.call-update) | async-done | bytes 65552 | tf_op jit(solution)/shard_map/psum | solution.py:103
  842.0 1.5 convolution_negate_fusion
  843.5 98.7 %all-gather.7.cloned.1.call-done = f32[16384,128]{1,0:T(8,128)} async-done(((f32[512,128]{1,0:T(8,128)}), f32[16384,128]{1,0:T(8,128)}) %all-gather.7.cloned.1.call-update) | async-done | bytes 8388624 | tf_op jit(solution)/shard_map/all_gather | solution.py:106
  942.2 5.0 fusion.49
  947.3 6.7 subtract_subtract_fusion
  (633 shorter events, 217.1 us)
Async XLA Ops:
  7.2 1.0 copy-start
  7.2 145.8 %all-reduce.5.cloned.1.call-start = ((), (), s32[]{:S(2)}) async-start(), calls=%async_computation | async-start | bytes 131072 | tf_op jit(solution)/shard_map/psum | solution.py:86
  9.4 245.6 %all-gather.9.cloned.1.call-start = ((), (), s32[]{:S(2)}) async-start(), calls=%async_computation.6 | async-start | bytes 2162688 | tf_op jit(solution)/shard_map/all_gather | solution.py:89
  167.8 674.2 %copy-start.4 = (f32[128,128]{1,0:T(8,128)}, f32[128,128]{1,0:T(8,128)S(1)}, u32[]{:S(2)}) copy-start(f32[128,128]{1,0:T(8,128)S(1)} %get-tuple-element.942) | copy-start | bytes 196612
  179.1 241.4 %all-reduce.9.cloned.1.call-start = ((), (), s32[]{:S(2)}) async-start(), calls=%async_computation.3 | async-start | bytes 131072 | tf_op jit(solution)/shard_map/psum | solution.py:11
  281.4 342.3 %all-gather.5.cloned.1.call-start = ((), (), s32[]{:S(2)}) async-start(), calls=%async_computation.1 | async-start | bytes 8650752 | tf_op jit(solution)/shard_map/all_gather | solution.py:98
  282.0 415.2 %all-reduce.7.cloned.1.call-start = ((), (), s32[]{:S(2)}) async-start(), calls=%async_computation.2 | async-start | bytes 524288 | tf_op jit(solution)/shard_map/psum | solution.py:101
  572.7 126.1 %copy-start.2 = (f32[512,128]{0,1:T(8,128)S(1)}, f32[512,128]{0,1:T(8,128)}, u32[]{:S(2)}) copy-start(f32[512,128]{0,1:T(8,128)} %get-tuple-element.943) | copy-start | bytes 786436
  631.3 208.2 %all-reduce.11.cloned.1.call-start = ((), (), s32[]{:S(2)}) async-start(), calls=%async_computation.4 | async-start | bytes 131072 | tf_op jit(solution)/shard_map/psum | solution.py:103
  699.9 242.3 %all-gather.7.cloned.1.call-start = ((), (), s32[]{:S(2)}) async-start(), calls=%async_computation.5 | async-start | bytes 8650752 | tf_op jit(solution)/shard_map/all_gather | solution.py:106
  841.9 105.3 %copy-start.3 = (f32[512,128]{1,0:T(8,128)S(1)}, f32[512,128]{1,0:T(8,128)}, u32[]{:S(2)}) copy-start(f32[512,128]{1,0:T(8,128)} %fusion.48) | copy-start | bytes 786436
  942.2 5.1 copy-start.1
Sparse Core Ops, SparseCore 0:
  12.0 140.8 all-reduce.4
  179.2 75.7 all-gather.8
  281.5 138.8 all-reduce.8
  423.5 100.0 all-gather.4
  631.4 65.7 all-reduce.6
  701.1 138.2 all-reduce.10
  842.6 99.5 all-gather.6
